TPU v7x, 32 devices: a whole 2x2x4 slice. The times are simulated.
32 devices in a mesh: dp: 16 (over z, x, core), mp: 2 (over y).
Axes of the slice: x: 2, y: 2, z: 4, core: 2. Of those that a mesh axis runs over, the one named last changes fastest.
Arguments:
- patches: bfloat16 [40960, 512], P(('dp', 'mp')), may hold values from -6 to 6
- cotangent: bfloat16 [40960, 512], P(('dp', 'mp')), may hold values from -6 to 6
- key_count: int32 [80], P('dp'), may hold values from 64 to 512, as said below
- w_qkv: float32 [3, 512, 512], P(None, None, 'mp')
- w_proj: float32 [512, 512], P('mp'), may hold values from -1 to 1
- w_up: float32 [512, 2048], P(None, 'mp')
- w_down: float32 [2048, 512], P('mp'), may hold values from -0.125 to 0.125
- qv_bias: float32 [2, 512], P(None, 'mp'), may hold values from -3 to 3
- up_bias: float32 [2048], P('mp'), may hold values from -3 to 3
- vec_params: float32 [6, 512], replicated
- first_qkv: float32 [3, 512, 512], P(None, None, 'mp'), may hold values from -0.00028163442 to 0.00028163442
- second_qkv: float32 [3, 512, 512], P(None, None, 'mp'), may hold values from 1.6815404e-08 to 6.6627074e-08
- first_proj: float32 [512, 512], P('mp'), may hold values from -0.00028163442 to 0.00028163442
- second_proj: float32 [512, 512], P('mp'), may hold values from 1.6815404e-08 to 6.6627074e-08
- first_up: float32 [512, 2048], P(None, 'mp'), may hold values from -0.00028163442 to 0.00028163442
- second_up: float32 [512, 2048], P(None, 'mp'), may hold values from 1.6815404e-08 to 6.6627074e-08
- first_down: float32 [2048, 512], P('mp'), may hold values from -0.00028163442 to 0.00028163442
- second_down: float32 [2048, 512], P('mp'), may hold values from 1.6815404e-08 to 6.6627074e-08
- first_qv_bias: float32 [2, 512], P(None, 'mp'), may hold values from -0.00056326884 to 0.00056326884
- second_qv_bias: float32 [2, 512], P(None, 'mp'), may hold values from 6.6627074e-08 to 2.665083e-07
- first_up_bias: float32 [2048], P('mp'), may hold values from -0.00056326884 to 0.00056326884
- second_up_bias: float32 [2048], P('mp'), may hold values from 9.518153e-09 to 3.8072614e-08
- first_vec: float32 [6, 512], replicated, may hold values from -0.00056326884 to 0.00056326884
- second_vec: float32 [6, 512], replicated, may hold values from 6.6627074e-08 to 2.665083e-07
Outputs:
- activations: bfloat16 [40960, 512], P(('dp', 'mp'))
- input_grad: float32 [40960, 512], P(('dp', 'mp'))
- grad_norm: float32 [], replicated
- qkv_new: float32 [3, 512, 512], P(None, None, 'mp')
- qkv_first: float32 [3, 512, 512], P(None, None, 'mp')
- qkv_second: float32 [3, 512, 512], P(None, None, 'mp')
- proj_new: float32 [512, 512], P('mp')
- proj_first: float32 [512, 512], P('mp')
- proj_second: float32 [512, 512], P('mp')
- up_new: float32 [512, 2048], P(None, 'mp')
- up_first: float32 [512, 2048], P(None, 'mp')
- up_second: float32 [512, 2048], P(None, 'mp')
- down_new: float32 [2048, 512], P('mp')
- down_first: float32 [2048, 512], P('mp')
- down_second: float32 [2048, 512], P('mp')
- qv_bias_new: float32 [2, 512], P(None, 'mp')
- qv_bias_first: float32 [2, 512], P(None, 'mp')
- qv_bias_second: float32 [2, 512], P(None, 'mp')
- up_bias_new: float32 [2048], P('mp')
- up_bias_first: float32 [2048], P('mp')
- up_bias_second: float32 [2048], P('mp')
- vec_new: float32 [6, 512], replicated
- vec_first: float32 [6, 512], replicated
- vec_second: float32 [6, 512], replicated
Inputs may be any that keep to these rules, and one draw needn't show every extreme that they name: `key_count`: each group's count is 512 (a full field) or between 64 and 512 // 4 (a small field padded); group 0 is full.
All inputs are finite; a program needn't handle non-finite values.
Results may differ from a plain program's by a relative error of at most 0.025.
Values may be sent and summed in bfloat16 or wider, within the bound.
A program may use at most 256 MiB of HBM per device.

v0:
```python
import jax
import jax.numpy as jnp
from jax import lax
from jax.sharding import PartitionSpec as P

HD = 32
ADAM_STEP = 10
NORM_EPS = 1e-06
BETA_FIRST = 0.9
BETA_SECOND = 0.95
ADAM_EPS = 1e-08
DECAY_RATE = 0.05
MATRIX_RATE = 0.1
VECTOR_RATE = 0.8
CLIP_NORM = 1.0
MASK_FILL = -1e30


def norm_forward(values, norm_gain, norm_shift):
    row_mean = jnp.mean(values, axis=-1, keepdims=True)
    centred = values - row_mean
    inverse = lax.rsqrt(jnp.mean(centred * centred, axis=-1, keepdims=True) + NORM_EPS)
    normed = centred * inverse
    return (normed * norm_gain + norm_shift, normed, inverse)


def norm_backward(grad_rows, normed, inverse, norm_gain):
    scaled = grad_rows * norm_gain
    centre_term = jnp.mean(scaled, axis=-1, keepdims=True)
    slope_term = jnp.mean(scaled * normed, axis=-1, keepdims=True)
    return inverse * (scaled - centre_term - normed * slope_term)


def exact_gelu(values):
    return jax.nn.gelu(values, approximate=False)


def key_mask(key_count, length):
    position = lax.broadcasted_iota(jnp.int32, (1, 1, 1, length), 3)
    return position < key_count[:, None, None, None]


def masked_scores(queries, key_rows, key_count):
    raw_scores = jnp.einsum(
        "sqhe,skhe->shqk", queries, key_rows, preferred_element_type=jnp.float32
    )
    scaled = raw_scores * queries.shape[-1] ** (-0.5)
    return jnp.where(key_mask(key_count, key_rows.shape[1]), scaled, MASK_FILL)


def attend_backward(queries, key_rows, value_rows, key_count, log_total, attended_grad):
    scores = masked_scores(queries, key_rows, key_count)
    probs = jnp.exp(scores - log_total)
    probs_low = probs.astype(jnp.bfloat16)
    probs_grad = jnp.einsum(
        "sqhe,skhe->shqk", attended_grad, value_rows, preferred_element_type=jnp.float32
    )
    score_grad = probs * (probs_grad - jnp.sum(probs_grad * probs, axis=-1, keepdims=True))
    visible = key_mask(key_count, key_rows.shape[1])
    raw_grad = jnp.where(visible, score_grad * queries.shape[-1] ** (-0.5), 0.0).astype(
        jnp.bfloat16
    )
    query_grad = jnp.einsum(
        "shqk,skhe->sqhe", raw_grad, key_rows, preferred_element_type=jnp.float32
    )
    key_grad = jnp.einsum("shqk,sqhe->skhe", raw_grad, queries, preferred_element_type=jnp.float32)
    value_grad = jnp.einsum(
        "shqk,sqhe->skhe", probs_low, attended_grad, preferred_element_type=jnp.float32
    )
    return jnp.stack([query_grad, key_grad, value_grad])


def own_slice(values, own_start, own_rows):
    return lax.dynamic_slice_in_dim(values, own_start, own_rows, 0)


def contract_rows(left, right):
    return lax.dot_general(
        left, right, (((0,), (0,)), ((), ())), preferred_element_type=jnp.float32
    )


def contract_cols(left, right):
    return lax.dot_general(
        left, right, (((1,), (1,)), ((), ())), preferred_element_type=jnp.float32
    )


def adam_update(weight, gradient, moment_one, moment_two, step_rate, decay_rate):
    first_new = BETA_FIRST * moment_one + (1.0 - BETA_FIRST) * gradient
    second_new = BETA_SECOND * moment_two + (1.0 - BETA_SECOND) * gradient * gradient
    first_hat = first_new / (1.0 - BETA_FIRST**ADAM_STEP)
    second_hat = second_new / (1.0 - BETA_SECOND**ADAM_STEP)
    weight_new = weight - step_rate * (
        first_hat / (jnp.sqrt(second_hat) + ADAM_EPS) + decay_rate * weight
    )
    return (weight_new, first_new, second_new)


def local(
    patches,
    cotangent,
    key_count,
    w_qkv,
    w_proj,
    w_up,
    w_down,
    qv_bias,
    up_bias,
    vec_params,
    first_qkv,
    second_qkv,
    first_proj,
    second_proj,
    first_up,
    second_up,
    first_down,
    second_down,
    first_qv_bias,
    second_qv_bias,
    first_up_bias,
    second_up_bias,
    first_vec,
    second_vec,
):
    own_rows = patches.shape[0]
    seq_count = key_count.shape[0]
    own_start = lax.axis_index("mp") * own_rows
    local_width = w_proj.shape[0]
    local_heads = local_width // HD
    own_grad = cotangent.astype(jnp.float32)
    qkv_low = w_qkv.astype(jnp.bfloat16)
    proj_low = w_proj.astype(jnp.bfloat16)
    up_low = w_up.astype(jnp.bfloat16)
    down_low = w_down.astype(jnp.bfloat16)
    gain_one, shift_one = (vec_params[0], vec_params[1])
    gain_two, shift_two = (vec_params[2], vec_params[3])
    proj_shift, down_shift = (vec_params[4], vec_params[5])
    qkv_shift = jnp.stack([qv_bias[0], jnp.zeros_like(qv_bias[0]), qv_bias[1]])[:, None, :]
    gathered, grad_all = (
        lax.all_gather(patches, "mp", axis=0, tiled=True),
        lax.all_gather(cotangent, "mp", axis=0, tiled=True),
    )
    whole_rows = gathered.astype(jnp.float32)
    normed_all, unit_one, inverse_one = norm_forward(whole_rows, gain_one, shift_one)
    norm_one = normed_all.astype(jnp.bfloat16)
    projected = (
        jnp.einsum("td,cde->cte", norm_one, qkv_low, preferred_element_type=jnp.float32) + qkv_shift
    )
    shaped = projected.astype(jnp.bfloat16).reshape(3, seq_count, -1, local_heads, HD)
    queries, key_rows, value_rows = (shaped[0], shaped[1], shaped[2])
    scores = masked_scores(queries, key_rows, key_count)
    top_score = jnp.max(scores, axis=-1, keepdims=True)
    log_total = top_score + jnp.log(jnp.sum(jnp.exp(scores - top_score), axis=-1, keepdims=True))
    probs_low = jnp.exp(scores - log_total).astype(jnp.bfloat16)
    attended = jnp.einsum(
        "shqk,skhe->sqhe", probs_low, value_rows, preferred_element_type=jnp.float32
    )
    attended_low = attended.astype(jnp.bfloat16).reshape(-1, local_width)
    proj_part = jnp.dot(attended_low, proj_low, preferred_element_type=jnp.float32)
    resid_all = whole_rows + lax.psum(proj_part, "mp") + proj_shift
    mid_all, unit_two, inverse_two = norm_forward(resid_all, gain_two, shift_two)
    norm_two = mid_all.astype(jnp.bfloat16)
    up_pre = jnp.dot(norm_two, up_low, preferred_element_type=jnp.float32) + up_bias
    hidden_full, gelu_pull = jax.vjp(exact_gelu, up_pre)
    hidden_low = hidden_full.astype(jnp.bfloat16)
    down_part = jnp.dot(hidden_low, down_low, preferred_element_type=jnp.float32)
    out_all = (
        resid_all + lax.psum(down_part.astype(jnp.bfloat16), "mp").astype(jnp.float32) + down_shift
    )
    block_out = own_slice(out_all, own_start, own_rows)
    activations = block_out.astype(jnp.bfloat16)
    down_grad = contract_rows(hidden_low, grad_all)
    hidden_grad = contract_cols(grad_all, down_low)
    up_grad_rows = gelu_pull(hidden_grad)[0].astype(jnp.bfloat16)
    up_grad = contract_rows(norm_two, up_grad_rows)
    up_bias_grad = jnp.sum(up_grad_rows.astype(jnp.float32), axis=0)
    mid_part = contract_cols(up_grad_rows, up_low)
    mid_all_grad = lax.psum(mid_part.astype(jnp.bfloat16), "mp").astype(jnp.float32)
    resid_all_grad = grad_all.astype(jnp.float32) + norm_backward(
        mid_all_grad, unit_two, inverse_two, gain_two
    )
    branch_low = resid_all_grad.astype(jnp.bfloat16)
    own_branch = own_slice(branch_low, own_start, own_rows)
    mid_grad = own_slice(mid_all_grad, own_start, own_rows)
    mid_unit = own_slice(unit_two, own_start, own_rows)
    proj_grad = contract_rows(attended_low, branch_low)
    attended_grad = (
        contract_cols(branch_low, proj_low)
        .astype(jnp.bfloat16)
        .reshape(seq_count, -1, local_heads, HD)
    )
    qkv_grads = attend_backward(queries, key_rows, value_rows, key_count, log_total, attended_grad)
    qkv_grad_rows = qkv_grads.reshape(3, -1, local_width).astype(jnp.bfloat16)
    qkv_grad = jnp.einsum(
        "td,cte->cde", norm_one, qkv_grad_rows, preferred_element_type=jnp.float32
    )
    qkv_grad_sums = jnp.sum(qkv_grad_rows.astype(jnp.float32), axis=1)
    qv_bias_grad = jnp.stack([qkv_grad_sums[0], qkv_grad_sums[2]])
    first_part = jnp.einsum(
        "cte,cde->td", qkv_grad_rows, qkv_low, preferred_element_type=jnp.float32
    )
    first_all = lax.psum(first_part.astype(jnp.bfloat16), "mp").astype(jnp.float32)
    input_all = resid_all_grad + norm_backward(first_all, unit_one, inverse_one, gain_one)
    input_grad = own_slice(input_all, own_start, own_rows)
    own_first_grad = own_slice(first_all, own_start, own_rows)
    own_unit_one = own_slice(unit_one, own_start, own_rows)
    vec_grad = jnp.stack(
        [
            jnp.sum(own_first_grad * own_unit_one, axis=0),
            jnp.sum(own_first_grad, axis=0),
            jnp.sum(mid_grad * mid_unit, axis=0),
            jnp.sum(mid_grad, axis=0),
            jnp.sum(own_branch.astype(jnp.float32), axis=0),
            jnp.sum(own_grad, axis=0),
        ]
    )
    summed = (
        lax.psum(qkv_grad.astype(jnp.bfloat16), "dp").astype(jnp.float32),
        lax.psum(proj_grad.astype(jnp.bfloat16), "dp").astype(jnp.float32),
        lax.psum(up_grad.astype(jnp.bfloat16), "dp").astype(jnp.float32),
        lax.psum(down_grad.astype(jnp.bfloat16), "dp").astype(jnp.float32),
        lax.psum(qv_bias_grad.astype(jnp.bfloat16), "dp").astype(jnp.float32),
        lax.psum(up_bias_grad.astype(jnp.bfloat16), "dp").astype(jnp.float32),
        lax.psum(vec_grad.astype(jnp.bfloat16), "dp").astype(jnp.float32),
    )
    split_square = jnp.float32(0.0)
    for gradient in summed[:6]:
        split_square = split_square + jnp.sum(gradient * gradient)
    vec_total, split_total = lax.psum((summed[6], split_square), "mp")
    grad_norm = jnp.sqrt(split_total + jnp.sum(vec_total * vec_total))
    factor = jnp.minimum(1.0, CLIP_NORM / (grad_norm + 1e-06))
    qkv_new, qkv_first, qkv_second = adam_update(
        w_qkv, summed[0] * factor, first_qkv, second_qkv, MATRIX_RATE, DECAY_RATE
    )
    proj_new, proj_first, proj_second = adam_update(
        w_proj, summed[1] * factor, first_proj, second_proj, MATRIX_RATE, DECAY_RATE
    )
    up_new, up_first, up_second = adam_update(
        w_up, summed[2] * factor, first_up, second_up, MATRIX_RATE, DECAY_RATE
    )
    down_new, down_first, down_second = adam_update(
        w_down, summed[3] * factor, first_down, second_down, MATRIX_RATE, DECAY_RATE
    )
    qvb_new, qvb_first, qvb_second = adam_update(
        qv_bias, summed[4] * factor, first_qv_bias, second_qv_bias, VECTOR_RATE, 0.0
    )
    upb_new, upb_first, upb_second = adam_update(
        up_bias, summed[5] * factor, first_up_bias, second_up_bias, VECTOR_RATE, 0.0
    )
    vec_new, vec_first, vec_second = adam_update(
        vec_params, vec_total * factor, first_vec, second_vec, VECTOR_RATE, 0.0
    )
    return (
        activations,
        input_grad,
        grad_norm,
        qkv_new,
        qkv_first,
        qkv_second,
        proj_new,
        proj_first,
        proj_second,
        up_new,
        up_first,
        up_second,
        down_new,
        down_first,
        down_second,
        qvb_new,
        qvb_first,
        qvb_second,
        upb_new,
        upb_first,
        upb_second,
        vec_new,
        vec_first,
        vec_second,
    )


def solution(mesh):
    return jax.shard_map(
        local,
        mesh=mesh,
        in_specs=(
            P(("dp", "mp"), None),
            P(("dp", "mp"), None),
            P("dp"),
            P(None, None, "mp"),
            P("mp", None),
            P(None, "mp"),
            P("mp", None),
            P(None, "mp"),
            P("mp"),
            P(),
            P(None, None, "mp"),
            P(None, None, "mp"),
            P("mp", None),
            P("mp", None),
            P(None, "mp"),
            P(None, "mp"),
            P("mp", None),
            P("mp", None),
            P(None, "mp"),
            P(None, "mp"),
            P("mp"),
            P("mp"),
            P(),
            P(),
        ),
        out_specs=(
            P(("dp", "mp"), None),
            P(("dp", "mp"), None),
            P(),
            P(None, None, "mp"),
            P(None, None, "mp"),
            P(None, None, "mp"),
            P("mp", None),
            P("mp", None),
            P("mp", None),
            P(None, "mp"),
            P(None, "mp"),
            P(None, "mp"),
            P("mp", None),
            P("mp", None),
            P("mp", None),
            P(None, "mp"),
            P(None, "mp"),
            P(None, "mp"),
            P("mp"),
            P("mp"),
            P("mp"),
            P(),
            P(),
            P(),
        ),
        check_vma=False,
    )
```

profile of v0, /device:TPU:0, one launch (start us, length us, event | category | flops | bytes accessed | tf_op | source)
XLA Modules:
  0.0 950.1 jit_solution(12365071723800339372)
XLA Ops:
  11.1 40.2 %all-gather.3.cloned.1.call-done = bf16[2560,512]{1,0:T(8,128)(2,1)} async-done(((bf16[1280,512]{1,0:T(8,128)(2,1)}), bf16[2560,512]{1,0:T(8,128)(2,1)}) %all-gather.3.cloned.1.call-update) | async-done | bytes 2621456 | tf_op jit(solution)/shard_map/all_gather | solution.py:141
  53.7 2.9 fusion.38
  56.6 3.2 fusion.40
  64.2 4.1 squeeze.10
  70.7 4.1 squeeze.11
  77.2 4.1 squeeze.9
  81.3 20.5 %fusion.2 = (f32[5,8,512]{2,1,0:T(8,128)S(1)}, f32[5,8,512,512]{2,3,1,0:T(8,128)}) fusion(pred[5,512]{1,0:T(8,128)(4,1)S(1)} %iota_compare_fusion, bf16[5,512,8,32]{1,0,3,2:T(8,128)(2,1)} %squeeze.11, bf16[5,512,8,32]{1,0,3,2:T(8,128)(2,1)} %squeeze.10), kind=kOutput, calls=%fused_computation.7 | convolution fusion | flops 702525440 | bytes 44648960 | tf_op jit(solution)/shard_map/sqhe,skhe->shqk/dot_general | solution.py:44
  101.7 17.9 %exponential_reduce_fusion = f32[5,8,512]{2,1,0:T(8,128)S(1)} fusion(f32[5,8,512,512]{2,3,1,0:T(8,128)} %get-tuple-element.135, f32[5,8,512]{2,1,0:T(8,128)S(1)} %get-tuple-element.134, pred[5,512]{1,0:T(8,128)(4,1)S(1)} %iota_compare_fusion), kind=kLoop, calls=%fused_computation.5 | loop fusion | flops 41922560 | bytes 42109440 | tf_op jit(solution)/shard_map/reduce_sum | solution.py:154
  119.7 19.6 %fusion.64 = bf16[5,512,8,32]{1,3,2,0:T(8,128)(2,1)} fusion(bf16[5,512,8,32]{1,0,3,2:T(8,128)(2,1)} %squeeze.9, f32[5,8,512,512]{2,3,1,0:T(8,128)} %get-tuple-element.135, f32[5,8,512]{2,1,0:T(8,128)S(1)} %log_add_fusion, pred[5,512]{1,0:T(8,128)(4,1)S(1)} %iota_compare_fusion), kind=kOutput, calls=%fused_computation.103 | convolution fusion | flops 713687040 | bytes 44648960 | tf_op jit(solution)/shard_map/shqk,skhe->sqhe/dot_general | solution.py:156
  143.2 3.2 fusion.98
  147.2 129.9 %all-reduce.9.cloned.1.call-done = f32[2560,512]{1,0:T(8,128)} async-done(((f32[2560,512]{1,0:T(8,128)}), f32[2560,512]{1,0:T(8,128)}) %all-reduce.9.cloned.1.call-update) | async-done | bytes 5242896 | tf_op jit(solution)/shard_map/psum | solution.py:161
  277.1 3.2 fusion.143
  285.3 26.6 %multiply_convert_fusion = (bf16[2560,1024]{1,0:T(8,128)(2,1)}, f32[2560,1024]{1,0:T(8,128)}, f32[2560,1024]{1,0:T(8,128)}) fusion(f32[1024]{0:T(1024)S(1)} %copy-done.48, f32[512,1024]{1,0:T(8,128)S(1)} %copy-done.29, f32[2560,512]{1,0:T(8,128)S(1)} %subtract_multiply_fusion, f32[512]{0:T(512)S(1)} %bitcast.72, f32[512]{0:T(512)S(1)} %bitcast.61), kind=kOutput, calls=%fused_computation.24 | convolution fusion | flops 2861826048 | bytes 33562624 | tf_op jit(solution)/shard_map/dot_general | solution.py:164
  311.9 5.8 all-gather.5.cloned.1.call-done
  317.8 12.5 %fusion.149 = (bf16[1024]{0:T(1024)(128)(2,1)}, bf16[2560,1024]{1,0:T(8,128)(2,1)S(1)}) fusion(f32[2560,1024]{1,0:T(8,128)} %get-tuple-element.113, bf16[2560,512]{1,0:T(8,128)(2,1)} %all-gather.5.cloned.1.call-done, f32[1024,512]{1,0:T(8,128)S(1)} %copy-done.25, f32[2560,1024]{1,0:T(8,128)} %get-tuple-element.136, f32[1024]{0:T(1024)S(1)} %copy-done.48), kind=kOutput, calls=%fused_computation.190 | convolution fusion | flops 2726820864 | bytes 30939136 | tf_op jit(solution)/shard_map/dot_general | solution.py:84
  332.7 4.4 convolution_convert_fusion
  337.2 7.3 convolution_convert_fusion.5
  344.5 6.4 convolution_convert_fusion.6
  350.8 60.7 %all-reduce.11.cloned.1.call-done = bf16[2560,512]{1,0:T(8,128)(2,1)} async-done(((bf16[2560,512]{1,0:T(8,128)(2,1)}), bf16[2560,512]{1,0:T(8,128)(2,1)}) %all-reduce.11.cloned.1.call-update) | async-done | bytes 2621456 | tf_op jit(solution)/shard_map/psum | solution.py:179
  411.6 5.1 multiply_reduce_fusion.4
  416.7 6.5 fusion.142
  427.9 16.6 %fusion.65 = bf16[5,512,8,32]{1,3,2,0:T(8,128)(2,1)S(1)} fusion(bf16[5,512,8,32]{1,0,3,2:T(8,128)(2,1)S(1)} %reshape.145, f32[5,8,512,512]{2,3,1,0:T(8,128)} %get-tuple-element.135, f32[5,8,512]{2,1,0:T(8,128)S(1)} %log_add_fusion, pred[5,512]{1,0:T(8,128)(4,1)S(1)} %iota_compare_fusion), kind=kOutput, calls=%fused_computation.104 | convolution fusion | flops 713687040 | bytes 44648960 | tf_op jit(solution)/shard_map/shqk,sqhe->skhe/dot_general | solution.py:67
  444.6 16.2 %fusion.75 = f32[5,8,512,512]{2,3,1,0:T(8,128)} fusion(bf16[5,512,8,32]{1,0,3,2:T(8,128)(2,1)S(1)} %reshape.145, bf16[5,512,8,32]{1,0,3,2:T(8,128)(2,1)S(1)} %copy-done.13), kind=kOutput, calls=%fused_computation.114 | convolution fusion | flops 671088640 | bytes 44564480 | tf_op jit(solution)/shard_map/sqhe,skhe->shqk/dot_general | solution.py:55
  460.8 54.2 %fusion.69 = bf16[5,512,8,32]{1,3,2,0:T(8,128)(2,1)} fusion(f32[5,8,512,512]{2,3,1,0:T(8,128)} %fusion.75, f32[5,8,512,512]{2,3,1,0:T(8,128)} %get-tuple-element.135, f32[5,8,512]{2,1,0:T(8,128)S(1)} %log_add_fusion, pred[5,512]{1,0:T(8,128)(4,1)S(1)} %iota_compare_fusion, bf16[5,512,8,32]{1,0,3,2:T(8,128)(2,1)} %squeeze.11), kind=kOutput, calls=%fused_computation.106 | convolution fusion | flops 797594112 | bytes 86592000 | tf_op jit(solution)/shard_map/shqk,skhe->sqhe/dot_general | solution.py:63
  515.0 53.4 %fusion.66 = bf16[5,512,8,32]{1,3,2,0:T(8,128)(2,1)} fusion(f32[5,8,512,512]{2,3,1,0:T(8,128)} %fusion.75, f32[5,8,512,512]{2,3,1,0:T(8,128)} %get-tuple-element.135, f32[5,8,512]{2,1,0:T(8,128)S(1)} %log_add_fusion, pred[5,512]{1,0:T(8,128)(4,1)S(1)} %iota_compare_fusion, bf16[5,512,8,32]{1,0,3,2:T(8,128)(2,1)S(1)} %copy-done.9), kind=kOutput, calls=%fused_computation.105 | convolution fusion | flops 797594112 | bytes 86592000 | tf_op jit(solution)/shard_map/shqk,sqhe->skhe/dot_general | solution.py:66
  577.5 3.7 copy.81
  581.1 4.1 stack.48
  585.2 2.6 copy.88
  587.9 5.6 fusion.73
  593.6 7.7 convolution_convert_fusion.1
  601.3 3.5 bitcast_convert_fusion
  604.9 3.0 copy.95
  609.5 3.0 copy.92
  612.5 3.0 copy.93
  617.2 2.6 convert_element_type.145
  622.9 74.7 %all-reduce.13.cloned.1.call-done = (bf16[3,512,256]{1,2,0:T(8,128)(2,1)}, bf16[256,512]{1,0:T(8,128)(2,1)}, bf16[512,1024]{1,0:T(8,128)(2,1)}, bf16[1024,512]{1,0:T(8,128)(2,1)}) async-done(((bf16[3,512,256]{1,2,0:T(8,128)(2,1)}, bf16[256,512]{1,0:T(8,128)(2,1)}, bf16[512,1024]{1,0:T(8,128)(2,1)}, bf16[1024,512]{1,0:T(8,128)(2,1)}), (bf16[3,512,256]{1,2,0:T(8,128)(2,1)}, bf16[256,512]{1,0:T(8,128)(2,1)}, ...) | async-done | bytes 3145744 | tf_op jit(solution)/shard_map/psum | solution.py:219
  708.8 121.4 %all-reduce.15.cloned.1.call-done = (bf16[2560,512]{1,0:T(8,128)(2,1)}, bf16[2560,512]{1,0:T(8,128)(2,1)}) async-done(((bf16[2560,512]{1,0:T(8,128)(2,1)}, bf16[2560,512]{1,0:T(8,128)(2,1)}), (bf16[2560,512]{1,0:T(8,128)(2,1)}, bf16[2560,512]{1,0:T(8,128)(2,1)})) %all-reduce.15.cloned.1.call-update) | async-done | bytes 5242896 | tf_op jit(solution)/shard_map/psum | solution.py:203
  830.2 2.6 convert_element_type.150
  832.9 2.5 fusion.72
  838.0 61.2 %all-reduce.1 = (bf16[6,512]{1,0:T(8,128)(2,1)S(1)}, bf16[2,256]{1,0:T(2,128)(2,1)S(1)}, bf16[1024]{0:T(1024)(128)(2,1)S(1)}) all-reduce(bf16[6,512]{1,0:T(8,128)(2,1)S(1)} %stack.59, bf16[2,256]{1,0:T(2,128)(2,1)S(1)} %pad_maximum_fusion.2, bf16[1024]{0:T(1024)(128)(2,1)S(1)} %copy-done.56), channel_id=1, replica_groups=mesh['dp'=16,'mp'=2] {'dp'}, use_global_device_ids=true, to_apply=%region_36.37 | all-reduce | flops 4608 | bytes 18432 | tf_op jit(solution)/shard_map/psum | solution.py:225
  901.7 7.8 all-reduce
  911.5 4.7 multiply_subtract_fusion.2
  916.2 3.1 copy.96
  919.5 3.1 copy.97
  924.2 3.8 fusion.45
  929.9 2.6 multiply_subtract_fusion.3
  932.6 4.0 multiply_subtract_fusion
  938.0 3.9 multiply_subtract_fusion.1
  (198 shorter events, 65.7 us)
Async XLA Ops:
  7.2 44.1 %all-gather.3.cloned.1.call-start = ((), (), s32[]{:S(2)}) async-start(), calls=%async_computation | async-start | bytes 3932160 | tf_op jit(solution)/shard_map/all_gather | solution.py:141
  7.9 269.2 %all-reduce.9.cloned.1.call-start = ((), (), s32[]{:S(2)}) async-start(), calls=%async_computation.1 | async-start | bytes 10485760 | tf_op jit(solution)/shard_map/psum | solution.py:161
  11.1 48.6 %copy-start.45 = (f32[1,512]{1,0:T(1,128)}, f32[1,512]{1,0:T(1,128)S(1)}, u32[]{:S(2)}) copy-start(f32[1,512]{1,0:T(1,128)S(1)} %get-tuple-element.128) | copy-start | bytes 6148
  11.1 48.6 %copy-start.54 = (f32[1,512]{1,0:T(1,128)}, f32[1,512]{1,0:T(1,128)S(1)}, u32[]{:S(2)}) copy-start(f32[1,512]{1,0:T(1,128)S(1)} %get-tuple-element.127) | copy-start | bytes 6148
  51.3 5.2 copy-start.34
  53.7 6.1 copy-start.37
  146.4 171.4 %all-gather.5.cloned.1.call-start = ((), (), s32[]{:S(2)}) async-start(), calls=%async_computation.2 | async-start | bytes 3932160 | tf_op jit(solution)/shard_map/all_gather | solution.py:142
  147.1 264.4 %all-reduce.11.cloned.1.call-start = ((), (), s32[]{:S(2)}) async-start(), calls=%async_computation.3 | async-start | bytes 5242880 | tf_op jit(solution)/shard_map/psum | solution.py:179
  285.3 32.4 %copy-start.25 = (f32[1024,512]{1,0:T(8,128)S(1)}, f32[1024,512]{1,0:T(8,128)}, u32[]{:S(2)}) copy-start(f32[1024,512]{1,0:T(8,128)} %param.30) | copy-start | bytes 6291460
  317.8 14.9 %copy-start.30 = (f32[512,1024]{1,0:T(8,128)S(1)}, f32[512,1024]{1,0:T(8,128)}, u32[]{:S(2)}) copy-start(f32[512,1024]{1,0:T(8,128)} %param.29) | copy-start | bytes 6291460
  337.1 7.4 slice-start
  337.1 360.6 %all-reduce.13.cloned.1.call-start = ((), (), s32[]{:S(2)}) async-start(), calls=%async_computation.4 | async-start | bytes 6291456 | tf_op jit(solution)/shard_map/psum | solution.py:219
  337.1 7.3 slice-start.1
  350.8 65.8 %copy-start.24 = (bf16[2560,512]{1,0:T(8,128)(2,1)S(1)}, bf16[2560,512]{1,0:T(8,128)(2,1)}, u32[]{:S(2)}) copy-start(bf16[2560,512]{1,0:T(8,128)(2,1)} %all-gather.5.cloned.1.call-done) | copy-start | bytes 7864324
  416.7 6.5 copy-start.8
  427.9 16.6 %copy-start.13 = (bf16[5,512,8,32]{1,0,3,2:T(8,128)(2,1)S(1)}, bf16[5,512,8,32]{1,0,3,2:T(8,128)(2,1)}, u32[]{:S(2)}) copy-start(bf16[5,512,8,32]{1,0,3,2:T(8,128)(2,1)} %squeeze.9) | copy-start | bytes 3932164
  460.8 54.2 %copy-start.9 = (bf16[5,512,8,32]{1,0,3,2:T(8,128)(2,1)S(1)}, bf16[5,512,8,32]{1,0,3,2:T(8,128)(2,1)}, u32[]{:S(2)}) copy-start(bf16[5,512,8,32]{1,0,3,2:T(8,128)(2,1)} %squeeze.10) | copy-start | bytes 3932164
  577.5 10.4 %copy-start.2 = (bf16[2560,512]{1,0:T(8,128)(2,1)S(1)}, bf16[2560,512]{1,0:T(8,128)(2,1)}, u32[]{:S(2)}) copy-start(bf16[2560,512]{1,0:T(8,128)(2,1)} %all-gather.3.cloned.1.call-done) | copy-start | bytes 7864324
  577.5 10.4 %copy-start.38 = (f32[2560]{0:T(1024)S(1)}, f32[2560]{0:T(1024)}, u32[]{:S(2)}) copy-start(f32[2560]{0:T(1024)} %copy-done.37) | copy-start | bytes 30724
  577.5 10.4 %copy-start.40 = (f32[2560]{0:T(1024)S(1)}, f32[2560]{0:T(1024)}, u32[]{:S(2)}) copy-start(f32[2560]{0:T(1024)} %copy-done.39) | copy-start | bytes 30724
  577.5 10.4 %copy-start.46 = (f32[1,512]{1,0:T(1,128)S(1)}, f32[1,512]{1,0:T(1,128)}, u32[]{:S(2)}) copy-start(f32[1,512]{1,0:T(1,128)} %copy-done.45) | copy-start | bytes 6148
  577.5 10.4 %copy-start.55 = (f32[1,512]{1,0:T(1,128)S(1)}, f32[1,512]{1,0:T(1,128)}, u32[]{:S(2)}) copy-start(f32[1,512]{1,0:T(1,128)} %copy-done.54) | copy-start | bytes 6148
  593.5 236.7 %all-reduce.15.cloned.1.call-start = ((), (), s32[]{:S(2)}) async-start(), calls=%async_computation.5 | async-start | bytes 10485760 | tf_op jit(solution)/shard_map/psum | solution.py:203
  593.5 7.7 copy-start.14
  593.5 7.7 copy-start.16
  593.5 7.7 copy-start.18
  593.6 7.7 copy-start.35
  830.2 5.3 slice-start.2
  835.5 76.0 %copy-start.10 = (f32[3,512,256]{1,2,0:T(8,128)S(1)}, f32[3,512,256]{1,2,0:T(8,128)}, u32[]{:S(2)}) copy-start(f32[3,512,256]{1,2,0:T(8,128)} %copy.95) | copy-start | bytes 4718596
  835.6 76.0 %copy-start.11 = (f32[3,512,256]{1,2,0:T(8,128)S(1)}, f32[3,512,256]{1,2,0:T(8,128)}, u32[]{:S(2)}) copy-start(f32[3,512,256]{1,2,0:T(8,128)} %copy.92) | copy-start | bytes 4718596
  916.2 6.3 copy-start.12
  916.2 8.0 copy-start.44
  919.4 8.6 copy-start.47
  919.4 8.6 copy-start.52
  919.4 8.6 copy-start.53
  919.4 9.2 copy-start.49
  919.4 9.2 copy-start.50
  919.4 9.2 copy-start.51
  919.4 9.8 %copy-start.41 = (f32[6,512]{1,0:T(8,128)S(1)}, f32[6,512]{1,0:T(8,128)}, u32[]{:S(2)}) copy-start(f32[6,512]{1,0:T(8,128)} %param.33) | copy-start | bytes 36868
  919.4 9.8 %copy-start.42 = (f32[6,512]{1,0:T(8,128)S(1)}, f32[6,512]{1,0:T(8,128)}, u32[]{:S(2)}) copy-start(f32[6,512]{1,0:T(8,128)} %param.46) | copy-start | bytes 36868
  919.4 9.8 %copy-start.43 = (f32[6,512]{1,0:T(8,128)S(1)}, f32[6,512]{1,0:T(8,128)}, u32[]{:S(2)}) copy-start(f32[6,512]{1,0:T(8,128)} %param.47) | copy-start | bytes 36868
  919.4 10.4 %copy-start.21 = (f32[256,512]{1,0:T(8,128)S(1)}, f32[256,512]{1,0:T(8,128)}, u32[]{:S(2)}) copy-start(f32[256,512]{1,0:T(8,128)} %param.28) | copy-start | bytes 1572868
  919.5 10.4 %copy-start.36 = (bf16[256,512]{1,0:T(8,128)(2,1)S(1)}, bf16[256,512]{1,0:T(8,128)(2,1)}, u32[]{:S(2)}) copy-start(bf16[256,512]{1,0:T(8,128)(2,1)} %get-tuple-element.86) | copy-start | bytes 786436
  922.6 9.9 %copy-start.23 = (bf16[1024,512]{1,0:T(8,128)(2,1)S(1)}, bf16[1024,512]{1,0:T(8,128)(2,1)}, u32[]{:S(2)}) copy-start(bf16[1024,512]{1,0:T(8,128)(2,1)} %get-tuple-element.88) | copy-start | bytes 3145732
  924.2 8.3 copy-start.26
  924.2 8.3 copy-start.27
  924.2 8.3 copy-start.28
  932.6 5.4 copy-start.33
  (20 other events, 70.3 us)
Sparse Core Ops, SparseCore 0:
  9.6 41.7 all-gather.2
  146.5 130.5 all-reduce.8
  278.7 39.0 all-gather.4
  337.2 74.3 all-reduce.10
  593.6 104.0 all-reduce.12
  700.6 129.5 all-reduce.14
where the time goes:
time: 961 us; the launch traced here: 950 us
  waiting for transfers between devices  434 us (45%)
  matrix products  263 us (27%)
  other arithmetic  88.8 us (9%)
  local copies, waits for them, and re-layouts  73 us (8%)
  blocking collectives  69.1 us (7%)
  between operations  21.5 us (2%)
    psum x1, waiting for transfers between devices, local(): resid_all = whole_rows + lax.psum(proj_part, 'mp') + proj_shift  130 us
    psum x1, waiting for transfers between devices, local(): lax.psum(first_part.astype(jnp.bfloat16), 'mp').astype(jnp.float32)  121 us
    psum x1, waiting for transfers between devices, local(): lax.psum(qkv_grad.astype(jnp.bfloat16), 'dp').astype(jnp.float32)  74.7 us
    psum x1, blocking collectives, local(): lax.psum(vec_grad.astype(jnp.bfloat16), 'dp').astype(jnp.float32)  61.2 us
    psum x1, waiting for transfers between devices, local(): lax.psum(mid_part.astype(jnp.bfloat16), 'mp').astype(jnp.float32)  60.7 us
    dot_general x1, matrix products, attend_backward(): jnp.einsum('shqk,skhe->sqhe', raw_grad, key_rows, preferred_element_type=...  54.2 us
    dot_general x1, matrix products, attend_backward(): jnp.einsum('shqk,sqhe->skhe', raw_grad, queries, preferred_element_type=j...  53.4 us
    all_gather x1, waiting for transfers between devices, local(): lax.all_gather(patches, 'mp', axis=0, tiled=True)  40.2 us
  transfers between devices with their start and end apart: 6, of which 6 were waited for; matrix products, arithmetic and copies ran while one was open for 9% of the time, Pallas kernels for 0%

commit v1 on v0

--- a/solution.py
+++ b/solution.py
@@ -14,6 +14,11 @@
 VECTOR_RATE = 0.8
 CLIP_NORM = 1.0
 MASK_FILL = -1e30
+
+
+def gather_and_add(value, name):
+    parts = lax.all_gather(value, name)
+    return jnp.sum(parts, axis=0)
 
 
 def norm_forward(values, norm_gain, norm_shift):
@@ -200,7 +205,7 @@
     first_part = jnp.einsum(
         "cte,cde->td", qkv_grad_rows, qkv_low, preferred_element_type=jnp.float32
     )
-    first_all = lax.psum(first_part.astype(jnp.bfloat16), "mp").astype(jnp.float32)
+    first_all = gather_and_add(first_part.astype(jnp.bfloat16), "mp").astype(jnp.float32)
     input_all = resid_all_grad + norm_backward(first_all, unit_one, inverse_one, gain_one)
     input_grad = own_slice(input_all, own_start, own_rows)
     own_first_grad = own_slice(first_all, own_start, own_rows)

time: 961 us -> 960 us (level)
    psum x1 -> x0, waiting for transfers between devices: 121 us -> none  [local(): lax.psum(first_part.astype(jnp.bfloat16), 'mp').astype(jnp.float32)]
    all_gather x0 -> x1, waiting for transfers between devices: none -> 57.9 us  [gather_and_add(): parts = lax.all_gather(value, name)]
    psum x1, waiting for transfers between devices: 60.7 us -> 115 us  [local(): lax.psum(mid_part.astype(jnp.bfloat16), 'mp').astype(jnp.float32)]
    unnamed x131 -> x123, local copies, waits for them, and re-layouts: 25 us -> 24.4 us
where the time goes in v1:
time: 960 us; the launch traced here: 950 us
  waiting for transfers between devices  429 us (45%)
  matrix products  263 us (27%)
  other arithmetic  94.1 us (10%)
  local copies, waits for them, and re-layouts  72.5 us (8%)
  blocking collectives  69.1 us (7%)
  between operations  21.5 us (2%)
    psum x1, waiting for transfers between devices, local(): resid_all = whole_rows + lax.psum(proj_part, 'mp') + proj_shift  130 us
    psum x1, waiting for transfers between devices, local(): lax.psum(mid_part.astype(jnp.bfloat16), 'mp').astype(jnp.float32)  115 us
    psum x1, waiting for transfers between devices, local(): lax.psum(qkv_grad.astype(jnp.bfloat16), 'dp').astype(jnp.float32)  78.2 us
    psum x1, blocking collectives, local(): lax.psum(vec_grad.astype(jnp.bfloat16), 'dp').astype(jnp.float32)  61.2 us
    all_gather x1, waiting for transfers between devices, gather_and_add(): parts = lax.all_gather(value, name)  57.9 us
    dot_general x1, matrix products, attend_backward(): jnp.einsum('shqk,skhe->sqhe', raw_grad, key_rows, preferred_element_type=...  54.4 us
    dot_general x1, matrix products, attend_backward(): jnp.einsum('shqk,sqhe->skhe', raw_grad, queries, preferred_element_type=j...  53.5 us
    all_gather x1, waiting for transfers between devices, local(): lax.all_gather(patches, 'mp', axis=0, tiled=True)  40.2 us
  transfers between devices with their start and end apart: 6, of which 6 were waited for; matrix products, arithmetic and copies ran while one was open for 9% of the time, Pallas kernels for 0%

profile of v1, /device:TPU:0, one launch (start us, length us, event | category | flops | bytes accessed | tf_op | source)
XLA Modules:
  0.0 949.6 jit_solution(5355681546725488832)
XLA Ops:
  11.1 40.2 %all-gather.5.cloned.1.call-done = bf16[2560,512]{1,0:T(8,128)(2,1)} async-done(((bf16[1280,512]{1,0:T(8,128)(2,1)}), bf16[2560,512]{1,0:T(8,128)(2,1)}) %all-gather.5.cloned.1.call-update) | async-done | bytes 2621456 | tf_op jit(solution)/shard_map/all_gather | solution.py:146
  53.7 2.9 fusion.38
  56.6 3.2 fusion.40
  64.2 4.1 squeeze.10
  70.7 4.1 squeeze.11
  77.2 4.1 squeeze.9
  81.3 20.5 %fusion.2 = (f32[5,8,512]{2,1,0:T(8,128)S(1)}, f32[5,8,512,512]{2,3,1,0:T(8,128)}) fusion(pred[5,512]{1,0:T(8,128)(4,1)S(1)} %iota_compare_fusion, bf16[5,512,8,32]{1,0,3,2:T(8,128)(2,1)} %squeeze.11, bf16[5,512,8,32]{1,0,3,2:T(8,128)(2,1)} %squeeze.10), kind=kOutput, calls=%fused_computation.7 | convolution fusion | flops 702525440 | bytes 44648960 | tf_op jit(solution)/shard_map/sqhe,skhe->shqk/dot_general | solution.py:49
  101.8 17.9 %exponential_reduce_fusion = f32[5,8,512]{2,1,0:T(8,128)S(1)} fusion(f32[5,8,512,512]{2,3,1,0:T(8,128)} %get-tuple-element.135, f32[5,8,512]{2,1,0:T(8,128)S(1)} %get-tuple-element.134, pred[5,512]{1,0:T(8,128)(4,1)S(1)} %iota_compare_fusion), kind=kLoop, calls=%fused_computation.5 | loop fusion | flops 41922560 | bytes 42109440 | tf_op jit(solution)/shard_map/reduce_sum | solution.py:159
  119.7 19.6 %fusion.64 = bf16[5,512,8,32]{1,3,2,0:T(8,128)(2,1)} fusion(bf16[5,512,8,32]{1,0,3,2:T(8,128)(2,1)} %squeeze.9, f32[5,8,512,512]{2,3,1,0:T(8,128)} %get-tuple-element.135, f32[5,8,512]{2,1,0:T(8,128)S(1)} %log_add_fusion, pred[5,512]{1,0:T(8,128)(4,1)S(1)} %iota_compare_fusion), kind=kOutput, calls=%fused_computation.103 | convolution fusion | flops 713687040 | bytes 44648960 | tf_op jit(solution)/shard_map/shqk,skhe->sqhe/dot_general | solution.py:161
  143.2 3.2 fusion.98
  147.2 129.9 %all-reduce.8.cloned.1.call-done = f32[2560,512]{1,0:T(8,128)} async-done(((f32[2560,512]{1,0:T(8,128)}), f32[2560,512]{1,0:T(8,128)}) %all-reduce.8.cloned.1.call-update) | async-done | bytes 5242896 | tf_op jit(solution)/shard_map/psum | solution.py:166
  277.1 3.2 fusion.143
  285.4 26.6 %multiply_convert_fusion = (bf16[2560,1024]{1,0:T(8,128)(2,1)}, f32[2560,1024]{1,0:T(8,128)}, f32[2560,1024]{1,0:T(8,128)}) fusion(f32[1024]{0:T(1024)S(1)} %copy-done.43, f32[512,1024]{1,0:T(8,128)S(1)} %copy-done.24, f32[2560,512]{1,0:T(8,128)S(1)} %subtract_multiply_fusion, f32[512]{0:T(512)S(1)} %bitcast.74, f32[512]{0:T(512)S(1)} %bitcast.63), kind=kOutput, calls=%fused_computation.24 | convolution fusion | flops 2861826048 | bytes 33562624 | tf_op jit(solution)/shard_map/dot_general | solution.py:169
  311.9 5.9 all-gather.7.cloned.1.call-done
  317.8 12.5 %fusion.149 = (bf16[1024]{0:T(1024)(128)(2,1)}, bf16[2560,1024]{1,0:T(8,128)(2,1)S(1)}) fusion(f32[2560,1024]{1,0:T(8,128)} %get-tuple-element.115, bf16[2560,512]{1,0:T(8,128)(2,1)} %all-gather.7.cloned.1.call-done, f32[1024,512]{1,0:T(8,128)S(1)} %copy-done.23, f32[2560,1024]{1,0:T(8,128)} %get-tuple-element.136, f32[1024]{0:T(1024)S(1)} %copy-done.43), kind=kOutput, calls=%fused_computation.190 | convolution fusion | flops 2726820864 | bytes 30939136 | tf_op jit(solution)/shard_map/dot_general | solution.py:89
  330.3 4.4 convolution_convert_fusion
  335.6 4.2 convolution_convert_fusion.1
  341.5 6.4 convolution_convert_fusion.5
  347.9 7.9 convolution_convert_fusion.6
  355.8 115.1 %all-reduce.12.cloned.1.call-done = (bf16[2560,512]{1,0:T(8,128)(2,1)}, bf16[2560,512]{1,0:T(8,128)(2,1)}) async-done(((bf16[2560,512]{1,0:T(8,128)(2,1)}, bf16[2560,512]{1,0:T(8,128)(2,1)}), (bf16[2560,512]{1,0:T(8,128)(2,1)}, bf16[2560,512]{1,0:T(8,128)(2,1)})) %all-reduce.12.cloned.1.call-update) | async-done | bytes 5242896 | tf_op jit(solution)/shard_map/psum | solution.py:184
  470.9 4.9 multiply_reduce_fusion.4
  475.8 6.5 fusion.141
  487.0 16.6 %fusion.65 = bf16[5,512,8,32]{1,3,2,0:T(8,128)(2,1)S(1)} fusion(bf16[5,512,8,32]{1,0,3,2:T(8,128)(2,1)S(1)} %reshape.145, f32[5,8,512,512]{2,3,1,0:T(8,128)} %get-tuple-element.135, f32[5,8,512]{2,1,0:T(8,128)S(1)} %log_add_fusion, pred[5,512]{1,0:T(8,128)(4,1)S(1)} %iota_compare_fusion), kind=kOutput, calls=%fused_computation.104 | convolution fusion | flops 713687040 | bytes 44648960 | tf_op jit(solution)/shard_map/shqk,sqhe->skhe/dot_general | solution.py:72
  503.6 16.2 %fusion.75 = f32[5,8,512,512]{2,3,1,0:T(8,128)} fusion(bf16[5,512,8,32]{1,0,3,2:T(8,128)(2,1)S(1)} %reshape.145, bf16[5,512,8,32]{1,0,3,2:T(8,128)(2,1)S(1)} %copy-done.14), kind=kOutput, calls=%fused_computation.114 | convolution fusion | flops 671088640 | bytes 44564480 | tf_op jit(solution)/shard_map/sqhe,skhe->shqk/dot_general | solution.py:60
  519.8 54.4 %fusion.69 = bf16[5,512,8,32]{1,3,2,0:T(8,128)(2,1)} fusion(f32[5,8,512,512]{2,3,1,0:T(8,128)} %fusion.75, f32[5,8,512,512]{2,3,1,0:T(8,128)} %get-tuple-element.135, f32[5,8,512]{2,1,0:T(8,128)S(1)} %log_add_fusion, pred[5,512]{1,0:T(8,128)(4,1)S(1)} %iota_compare_fusion, bf16[5,512,8,32]{1,0,3,2:T(8,128)(2,1)} %squeeze.11), kind=kOutput, calls=%fused_computation.106 | convolution fusion | flops 797594112 | bytes 86592000 | tf_op jit(solution)/shard_map/shqk,skhe->sqhe/dot_general | solution.py:68
  574.2 53.5 %fusion.66 = bf16[5,512,8,32]{1,3,2,0:T(8,128)(2,1)} fusion(f32[5,8,512,512]{2,3,1,0:T(8,128)} %fusion.75, f32[5,8,512,512]{2,3,1,0:T(8,128)} %get-tuple-element.135, f32[5,8,512]{2,1,0:T(8,128)S(1)} %log_add_fusion, pred[5,512]{1,0:T(8,128)(4,1)S(1)} %iota_compare_fusion, bf16[5,512,8,32]{1,0,3,2:T(8,128)(2,1)S(1)} %copy-done.10), kind=kOutput, calls=%fused_computation.105 | convolution fusion | flops 797594112 | bytes 86592000 | tf_op jit(solution)/shard_map/shqk,sqhe->skhe/dot_general | solution.py:71
  636.8 3.7 copy.81
  640.5 4.1 stack.48
  644.6 2.6 copy.88
  647.2 5.6 fusion.73
  652.9 6.3 bitcast_convert_fusion
  659.2 3.0 copy.95
  663.8 3.1 copy.92
  666.9 3.0 copy.93
  670.0 2.7 convert_element_type.147
  678.8 78.2 %all-reduce.10.cloned.1.call-done = (bf16[3,512,256]{1,2,0:T(8,128)(2,1)}, bf16[256,512]{1,0:T(8,128)(2,1)}, bf16[512,1024]{1,0:T(8,128)(2,1)}, bf16[1024,512]{1,0:T(8,128)(2,1)}) async-done(((bf16[3,512,256]{1,2,0:T(8,128)(2,1)}, bf16[256,512]{1,0:T(8,128)(2,1)}, bf16[512,1024]{1,0:T(8,128)(2,1)}, bf16[1024,512]{1,0:T(8,128)(2,1)}), (bf16[3,512,256]{1,2,0:T(8,128)(2,1)}, bf16[256,512]{1,0:T(8,128)(2,1)}, ...) | async-done | bytes 3145744 | tf_op jit(solution)/shard_map/psum | solution.py:224
  765.2 2.5 fusion.51
  768.4 57.9 %all-gather.9.cloned.1.call-done = bf16[5120,512]{1,0:T(8,128)(2,1)} async-done(((bf16[2560,512]{1,0:T(8,128)(2,1)}), bf16[5120,512]{1,0:T(8,128)(2,1)}) %all-gather.9.cloned.1.call-update) | async-done | bytes 5242896 | tf_op jit(solution)/shard_map/all_gather | solution.py:20
  826.3 5.7 reduce_sum.248
  832.1 2.6 convert_element_type.152
  839.8 61.2 %all-reduce.1 = (bf16[6,512]{1,0:T(8,128)(2,1)S(1)}, bf16[2,256]{1,0:T(2,128)(2,1)S(1)}, bf16[1024]{0:T(1024)(128)(2,1)S(1)}) all-reduce(bf16[6,512]{1,0:T(8,128)(2,1)S(1)} %stack.59, bf16[2,256]{1,0:T(2,128)(2,1)S(1)} %pad_maximum_fusion.2, bf16[1024]{0:T(1024)(128)(2,1)S(1)} %copy-done.51), channel_id=1, replica_groups=mesh['dp'=16,'mp'=2] {'dp'}, use_global_device_ids=true, to_apply=%region_36.37 | all-reduce | flops 4608 | bytes 18432 | tf_op jit(solution)/shard_map/psum | solution.py:230
  903.5 7.8 all-reduce
  913.4 4.7 multiply_subtract_fusion.2
  918.2 3.2 copy.96
  921.4 3.1 copy.97
  928.0 2.6 multiply_subtract_fusion.3
  930.6 6.8 multiply_subtract_fusion
  937.5 3.9 multiply_subtract_fusion.1
  (191 shorter events, 66.1 us)
Async XLA Ops:
  7.2 44.1 %all-gather.5.cloned.1.call-start = ((), (), s32[]{:S(2)}) async-start(), calls=%async_computation | async-start | bytes 3932160 | tf_op jit(solution)/shard_map/all_gather | solution.py:146
  7.9 269.2 %all-reduce.8.cloned.1.call-start = ((), (), s32[]{:S(2)}) async-start(), calls=%async_computation.1 | async-start | bytes 10485760 | tf_op jit(solution)/shard_map/psum | solution.py:166
  11.1 48.6 %copy-start.40 = (f32[1,512]{1,0:T(1,128)}, f32[1,512]{1,0:T(1,128)S(1)}, u32[]{:S(2)}) copy-start(f32[1,512]{1,0:T(1,128)S(1)} %get-tuple-element.128) | copy-start | bytes 6148
  11.1 48.6 %copy-start.49 = (f32[1,512]{1,0:T(1,128)}, f32[1,512]{1,0:T(1,128)S(1)}, u32[]{:S(2)}) copy-start(f32[1,512]{1,0:T(1,128)S(1)} %get-tuple-element.127) | copy-start | bytes 6148
  51.3 5.2 copy-start.1
  51.3 5.2 copy-start.29
  53.7 6.1 copy-start.32
  146.4 171.4 %all-gather.7.cloned.1.call-start = ((), (), s32[]{:S(2)}) async-start(), calls=%async_computation.2 | async-start | bytes 3932160 | tf_op jit(solution)/shard_map/all_gather | solution.py:147
  147.2 323.7 %all-reduce.12.cloned.1.call-start = ((), (), s32[]{:S(2)}) async-start(), calls=%async_computation.5 | async-start | bytes 10485760 | tf_op jit(solution)/shard_map/psum | solution.py:184
  285.4 32.4 %copy-start.23 = (f32[1024,512]{1,0:T(8,128)S(1)}, f32[1024,512]{1,0:T(8,128)}, u32[]{:S(2)}) copy-start(f32[1024,512]{1,0:T(8,128)} %param.30) | copy-start | bytes 6291460
  317.8 12.5 %copy-start.25 = (f32[512,1024]{1,0:T(8,128)S(1)}, f32[512,1024]{1,0:T(8,128)}, u32[]{:S(2)}) copy-start(f32[512,1024]{1,0:T(8,128)} %param.29) | copy-start | bytes 6291460
  330.3 4.4 copy-start.53
  330.3 5.3 copy-start.52
  339.8 417.3 %all-reduce.10.cloned.1.call-start = ((), (), s32[]{:S(2)}) async-start(), calls=%async_computation.4 | async-start | bytes 6291456 | tf_op jit(solution)/shard_map/psum | solution.py:224
  470.9 4.9 copy-start.6
  475.8 6.5 copy-start.9
  487.0 16.6 %copy-start.14 = (bf16[5,512,8,32]{1,0,3,2:T(8,128)(2,1)S(1)}, bf16[5,512,8,32]{1,0,3,2:T(8,128)(2,1)}, u32[]{:S(2)}) copy-start(bf16[5,512,8,32]{1,0,3,2:T(8,128)(2,1)} %squeeze.9) | copy-start | bytes 3932164
  519.8 54.4 %copy-start.10 = (bf16[5,512,8,32]{1,0,3,2:T(8,128)(2,1)S(1)}, bf16[5,512,8,32]{1,0,3,2:T(8,128)(2,1)}, u32[]{:S(2)}) copy-start(bf16[5,512,8,32]{1,0,3,2:T(8,128)(2,1)} %squeeze.10) | copy-start | bytes 3932164
  636.8 10.4 %copy-start.2 = (bf16[2560,512]{1,0:T(8,128)(2,1)S(1)}, bf16[2560,512]{1,0:T(8,128)(2,1)}, u32[]{:S(2)}) copy-start(bf16[2560,512]{1,0:T(8,128)(2,1)} %all-gather.5.cloned.1.call-done) | copy-start | bytes 7864324
  636.8 10.4 %copy-start.33 = (f32[2560]{0:T(1024)S(1)}, f32[2560]{0:T(1024)}, u32[]{:S(2)}) copy-start(f32[2560]{0:T(1024)} %copy-done.32) | copy-start | bytes 30724
  636.8 10.4 %copy-start.35 = (f32[2560]{0:T(1024)S(1)}, f32[2560]{0:T(1024)}, u32[]{:S(2)}) copy-start(f32[2560]{0:T(1024)} %copy-done.34) | copy-start | bytes 30724
  636.8 10.4 %copy-start.41 = (f32[1,512]{1,0:T(1,128)S(1)}, f32[1,512]{1,0:T(1,128)}, u32[]{:S(2)}) copy-start(f32[1,512]{1,0:T(1,128)} %copy-done.40) | copy-start | bytes 6148
  636.8 10.4 %copy-start.50 = (f32[1,512]{1,0:T(1,128)S(1)}, f32[1,512]{1,0:T(1,128)}, u32[]{:S(2)}) copy-start(f32[1,512]{1,0:T(1,128)} %copy-done.49) | copy-start | bytes 6148
  652.8 173.5 %all-gather.9.cloned.1.call-start = ((), (), s32[]{:S(2)}) async-start(), calls=%async_computation.3 | async-start | bytes 7864320 | tf_op jit(solution)/shard_map/all_gather | solution.py:20
  670.0 5.4 copy-start.16
  670.0 5.4 copy-start.17
  672.7 4.3 copy-start.31
  672.8 4.3 copy-start.39
  832.1 5.3 slice-start.2
  837.4 76.0 %copy-start.11 = (f32[3,512,256]{1,2,0:T(8,128)S(1)}, f32[3,512,256]{1,2,0:T(8,128)}, u32[]{:S(2)}) copy-start(f32[3,512,256]{1,2,0:T(8,128)} %copy.95) | copy-start | bytes 4718596
  837.4 76.0 %copy-start.12 = (f32[3,512,256]{1,2,0:T(8,128)S(1)}, f32[3,512,256]{1,2,0:T(8,128)}, u32[]{:S(2)}) copy-start(f32[3,512,256]{1,2,0:T(8,128)} %copy.92) | copy-start | bytes 4718596
  918.1 6.4 copy-start.13
  918.1 8.0 copy-start.42
  918.1 8.0 copy-start.47
  918.1 8.0 copy-start.48
  918.1 8.6 copy-start.44
  918.1 8.6 copy-start.45
  918.1 8.6 copy-start.46
  918.1 9.2 copy-start.36
  918.1 9.2 copy-start.37
  918.2 9.2 copy-start.38
  918.2 9.8 %copy-start.19 = (f32[256,512]{1,0:T(8,128)S(1)}, f32[256,512]{1,0:T(8,128)}, u32[]{:S(2)}) copy-start(f32[256,512]{1,0:T(8,128)} %param.28) | copy-start | bytes 1572868
  918.2 9.8 %copy-start.30 = (bf16[256,512]{1,0:T(8,128)(2,1)S(1)}, bf16[256,512]{1,0:T(8,128)(2,1)}, u32[]{:S(2)}) copy-start(bf16[256,512]{1,0:T(8,128)(2,1)} %get-tuple-element.86) | copy-start | bytes 786436
  921.4 9.2 copy-start.21
  930.6 6.9 copy-start.20
  930.6 6.9 copy-start.26
  930.6 6.9 copy-start.27
  930.6 6.9 copy-start.28
  (16 other events, 45.6 us)
Sparse Core Ops, SparseCore 0:
  9.6 41.7 all-gather.4
  146.6 130.5 all-reduce.7
  278.8 39.0 all-gather.6
  339.9 130.8 all-reduce.11
  652.9 104.0 all-reduce.9
  759.0 67.2 all-gather.8
